TPU v7x, 256 devices: a whole 4x4x8 slice. The times are simulated.
256 devices in a mesh: seq: 128 (over y, z, x_hi, core), ch: 2 (over x_lo).
Axes of the slice: x: 4 (x_hi: 2, x_lo: 2; x = x_hi * 2 + x_lo), y: 4, z: 8, core: 2. Of those that a mesh axis runs over, the one named last changes fastest.
Arguments:
- qkv: bfloat16 [3, 8192, 16384], P(None, 'ch', 'seq'), parts along dimension 1, may hold values from -6 to 6
- short_filter: float32 [3, 3, 8192], P(None, None, 'ch'), parts along dimension 2, may hold values from -3 to 3
- decay_rate: float32 [8192, 16], P('ch'), parts along dimension 0, may hold values from 1.5258789e-05 to 0.025
- residue: float32 [8192, 16], P('ch'), parts along dimension 0, may hold values from -2 to 2
- skip: float32 [8192], P('ch'), parts along dimension 0, may hold values from 0.1 to 1.9
Outputs:
- output: bfloat16 [8192, 16384], P('ch', 'seq'), parts along dimension 0
There are 2 independent parts, one for each index of `ch`. A program takes and returns all parts, laid end to end along the dimension named above; each array names one. Nothing has to cross between parts.
All inputs are finite; a program needn't handle non-finite values.
Results may differ from a plain program's by a relative error of at most 0.0057.
Values may be sent and summed in bfloat16 or wider, within the bound.
A program may use at most 256 MiB of HBM per device.

v0:
```python
import functools

import jax
import jax.numpy as jnp
from jax import lax
from jax.experimental import pallas as pl
from jax.experimental.pallas import tpu as pltpu
from jax.sharding import PartitionSpec as P

MODES = 16
SHORT = 3
MESH = pl.DeviceIdType.MESH
LANES = 128
CHUNKS = 8
STEPS = 16
F32 = jnp.float32
BF16 = jnp.bfloat16


def cols(block):
    return pl.ds(pl.multiple_of(block * LANES, LANES), LANES)


def wide(row):
    return jnp.broadcast_to(row, (CHUNKS, LANES))


def rounded(value):
    return value.astype(BF16).astype(F32)


def one_minus_exp(x):
    series = 1.0 - x * (1.0 / 7.0)
    for k in (6, 5, 4, 3, 2):
        series = 1.0 - x * (1.0 / k) * series
    return jnp.where(x < 0.25, x * series, 1.0 - jnp.exp(-x))


def kernel(
    n,
    x_hbm,
    taps_hbm,
    rate_hbm,
    residue_hbm,
    skip_hbm,
    out_ref,
    xv,
    taps,
    rate,
    residue,
    skip,
    decay,
    decay14,
    decay15,
    gated,
    states,
    first,
    feat0,
    halo_out,
    halo_in,
    weights,
    near_taps,
    near,
    ends_out,
    ends_in,
    starts_out,
    starts_in,
    load_sems,
    sems,
    own_sem,
):
    me = lax.axis_index("seq")
    blocks = x_hbm.shape[1] // LANES
    parts = n // blocks
    rows = MODES // parts
    following = lax.rem(me + 1, n)

    small = [(rate_hbm, rate), (taps_hbm, taps), (residue_hbm, residue), (skip_hbm, skip)]
    loads = [
        pltpu.make_async_copy(src, dst, load_sems.at[i]) for i, (src, dst) in enumerate(small)
    ]
    loads.append(pltpu.make_async_copy(x_hbm, xv, load_sems.at[len(small)]))
    for load in loads:
        load.start()

    barrier = pltpu.get_barrier_semaphore()

    def greet(i, carry):
        pl.semaphore_signal(
            barrier, inc=1, device_id={"seq": lax.rem(me + i, n)}, device_id_type=MESH
        )
        return carry

    lax.fori_loop(1, n, greet, 0)

    sub = lax.broadcasted_iota(jnp.int32, (CHUNKS, LANES), 0)
    top = sub == 0
    place = lax.broadcasted_iota(jnp.int32, (LANES, LANES), 0)
    token = lax.broadcasted_iota(jnp.int32, (LANES, LANES), 1)
    spread = jnp.where(
        token == lax.rem(place, CHUNKS) * STEPS + lax.div(place, CHUNKS), 1.0, 0.0
    ).astype(BF16)

    loads[0].wait()

    def prepare(block, carry):
        c = cols(block)
        r = rate[:, c]
        decay[:, c] = jnp.exp(-r)
        decay14[:, c] = jnp.exp(-14.0 * r)
        decay15[:, c] = jnp.exp(-15.0 * r)
        return carry

    lax.fori_loop(0, blocks, prepare, 0)

    for load in loads[1:]:
        load.wait()

    def local(block, carry):
        c = cols(block)
        feats = []
        halo_rows = jnp.zeros((CHUNKS, LANES), F32)
        for stream in range(3):
            moved = lax.dot_general(
                spread,
                xv[stream, c, :],
                (((1,), (1,)), ((), ())),
                preferred_element_type=F32,
            )
            v = [moved[j * CHUNKS : (j + 1) * CHUNKS] for j in range(STEPS)]
            for k in range(2):
                row = 2 * stream + k
                halo_rows = jnp.where(
                    sub == row, pltpu.roll(v[14 + k], row + 1, 0), halo_rows
                )
            back1 = jnp.where(top, 0.0, pltpu.roll(v[15], 1, 0))
            back2 = jnp.where(top, 0.0, pltpu.roll(v[14], 1, 0))
            v = [back2, back1] + v
            f = [wide(taps[k, pl.ds(stream, 1), c]) for k in range(3)]
            feat = [f[0] * v[j + 2] + f[1] * v[j + 1] + f[2] * v[j] for j in range(STEPS)]
            if stream == 0:
                for j in range(STEPS):
                    feat0[j * CHUNKS : (j + 1) * CHUNKS, c] = feat[j]
            else:
                for k in range(2):
                    at = (2 * (stream - 1) + k) * CHUNKS
                    first[at : at + CHUNKS, c] = feat[k]
                feats.append(feat)
        halo_out[:, c] = halo_rows.astype(BF16)
        g = [rounded(feats[0][j] * feats[1][j]) for j in range(STEPS)]
        for j in range(STEPS):
            gated[j * CHUNKS : (j + 1) * CHUNKS, c] = g[j]
        for mode in range(MODES):
            a = wide(decay[pl.ds(mode, 1), c])
            state = g[0]
            for j in range(1, STEPS):
                state = a * state + g[j]
            states[mode * CHUNKS : (mode + 1) * CHUNKS, c] = state
        return carry

    lax.fori_loop(0, blocks, local, 0)

    pl.semaphore_wait(barrier, n - 1)
    halo = pltpu.make_async_remote_copy(
        src_ref=halo_out,
        dst_ref=halo_in,
        send_sem=sems.at[0],
        recv_sem=sems.at[1],
        device_id={"seq": following},
        device_id_type=MESH,
    )
    halo.start()

    def tables(block, carry):
        c = cols(block)
        r = rate[:, c]
        a = decay[:, c]
        w = residue[:, c] * jnp.sqrt(one_minus_exp(2.0 * r))
        direct = skip[pl.ds(block, 1), :]
        for j in range(STEPS):
            near_taps[pl.ds(j, 1), c] = jnp.sum(w, axis=0, keepdims=True) + direct
            direct = 0.0
            w = w * a
            weights[j * MODES : (j + 1) * MODES, c] = w
        return carry

    lax.fori_loop(0, blocks, tables, 0)
    halo.wait()

    late = (CHUNKS - 1 - sub).astype(F32) * float(-STEPS)

    def finish(block, carry):
        c = cols(block)
        h = jnp.where(me == 0, 0.0, halo_in[:, c].astype(F32))

        def add_first(stream):
            f1 = taps[1, pl.ds(stream, 1), c]
            f2 = taps[2, pl.ds(stream, 1), c]
            h2 = h[2 * stream : 2 * stream + 1]
            h1 = h[2 * stream + 1 : 2 * stream + 2]
            return [
                jnp.where(top, wide(f1 * h1 + f2 * h2), 0.0),
                jnp.where(top, wide(f2 * h1), 0.0),
            ]

        more = [add_first(stream) for stream in range(3)]
        change = []
        for k in range(2):
            at = slice(k * CHUNKS, (k + 1) * CHUNKS)
            feat0[at, c] = feat0[at, c] + more[0][k]
            one = first[k * CHUNKS : (k + 1) * CHUNKS, c] + more[1][k]
            two = first[(2 + k) * CHUNKS : (3 + k) * CHUNKS, c] + more[2][k]
            g = rounded(one * two)
            change.append(g - gated[at, c])
            gated[at, c] = g
        sums = []
        for mode in range(MODES):
            at = slice(mode * CHUNKS, (mode + 1) * CHUNKS)
            state = (
                states[at, c]
                + wide(decay15[pl.ds(mode, 1), c]) * change[0]
                + wide(decay14[pl.ds(mode, 1), c]) * change[1]
            )
            states[at, c] = state
            sums.append(
                jnp.sum(
                    state * jnp.exp(wide(rate[pl.ds(mode, 1), c]) * late), axis=0, keepdims=True
                )
            )
        for part in range(parts):
            ends_out[block * parts + part] = jnp.concatenate(
                sums[part * rows : (part + 1) * rows], axis=0
            ).astype(BF16)
        return carry

    lax.fori_loop(0, blocks, finish, 0)

    def exchange(src, dst, send_sem, recv_sem):
        def one(i, carry):
            k = lax.rem(me + i, n)
            pltpu.make_async_remote_copy(
                src_ref=src.at[k],
                dst_ref=dst.at[me],
                send_sem=sems.at[send_sem],
                recv_sem=sems.at[recv_sem],
                device_id={"seq": k},
                device_id_type=MESH,
            ).start()
            return carry

        lax.fori_loop(1, n, one, 0)
        own = pltpu.make_async_copy(src.at[me], dst.at[me], own_sem.at[0])
        own.start()
        others = pltpu.make_async_remote_copy(
            src_ref=src.at[pl.ds(0, n - 1)],
            dst_ref=dst.at[pl.ds(0, n - 1)],
            send_sem=sems.at[send_sem],
            recv_sem=sems.at[recv_sem],
            device_id={"seq": following},
            device_id_type=MESH,
        )
        return own, others

    own, others = exchange(ends_out, ends_in, 2, 3)

    def inside(block, carry):
        c = cols(block)
        g = [gated[j * CHUNKS : (j + 1) * CHUNKS, c] for j in range(STEPS)]
        taps_here = [wide(near_taps[pl.ds(j, 1), c]) for j in range(STEPS)]
        for j in range(STEPS):
            total = taps_here[0] * g[j]
            for i in range(1, j + 1):
                total = total + taps_here[i] * g[j - i]
            near[j * CHUNKS : (j + 1) * CHUNKS, c] = total
        for mode in range(MODES):
            at = slice(mode * CHUNKS, (mode + 1) * CHUNKS)
            step = jnp.exp(wide(rate[pl.ds(mode, 1), c]) * float(-STEPS))
            state = states[at, c]
            for shift in (1, 2, 4):
                state = state + jnp.where(sub < shift, 0.0, step * pltpu.roll(state, shift, 0))
                step = step * step
            states[at, c] = jnp.where(top, 0.0, pltpu.roll(state, 1, 0))
        return carry

    lax.fori_loop(0, blocks, inside, 0)

    mine = lax.div(me, parts)
    part = lax.rem(me, parts)
    r = rate[:, cols(mine)]
    pick = r[0:rows]
    for k in range(1, parts):
        pick = jnp.where(part == k, r[k * rows : (k + 1) * rows], pick)
    across = jnp.exp(pick * float(-LANES))

    own.wait()
    others.wait_recv()

    def carry_on(source, entering):
        starts_out[source] = entering.astype(BF16)
        return across * entering + ends_in[source].astype(F32)

    lax.fori_loop(0, n, carry_on, jnp.zeros((rows, LANES), F32), unroll=8)
    others.wait_send()
    own, others = exchange(starts_out, starts_in, 4, 5)
    own.wait()
    others.wait_recv()

    early = sub.astype(F32) * float(-STEPS)

    def final(block, carry):
        c = cols(block)
        entering = []
        for mode in range(MODES):
            at = slice(mode * CHUNKS, (mode + 1) * CHUNKS)
            if mode % rows == 0:
                group = starts_in[block * parts + mode // rows].astype(F32)
            row = mode % rows
            entering.append(
                states[at, c]
                + wide(group[row : row + 1]) * jnp.exp(wide(rate[pl.ds(mode, 1), c]) * early)
            )
        results = []
        for j in range(STEPS):
            total = near[j * CHUNKS : (j + 1) * CHUNKS, c]
            for mode in range(MODES):
                total = total + wide(weights[pl.ds(j * MODES + mode, 1), c]) * entering[mode]
            results.append(feat0[j * CHUNKS : (j + 1) * CHUNKS, c] * rounded(total))
        turned = jnp.concatenate(results, axis=0).T.astype(BF16)
        out_ref[c, :] = jnp.dot(turned, spread, preferred_element_type=F32).astype(BF16)
        return carry

    lax.fori_loop(0, blocks, final, 0)
    others.wait_send()


def body(n, qkv, short_filter, decay_rate, residue, skip):
    channels, width = qkv.shape[1:]
    blocks = channels // LANES
    parts = n // blocks
    rows = MODES // parts
    anywhere = pl.BlockSpec(memory_space=pl.ANY)
    full = (LANES, channels)
    packet = (n, rows, LANES)
    return pl.pallas_call(
        functools.partial(kernel, n),
        out_shape=jax.ShapeDtypeStruct((channels, width), BF16),
        in_specs=[anywhere] * 5,
        out_specs=pl.BlockSpec(memory_space=pltpu.VMEM),
        scratch_shapes=[
            pltpu.VMEM(qkv.shape, BF16),
            pltpu.VMEM(short_filter.shape, F32),
            pltpu.VMEM((MODES, channels), F32),
            pltpu.VMEM((MODES, channels), F32),
            pltpu.VMEM((blocks, LANES), F32),
            pltpu.VMEM((MODES, channels), F32),
            pltpu.VMEM((MODES, channels), F32),
            pltpu.VMEM((MODES, channels), F32),
            pltpu.VMEM(full, F32),
            pltpu.VMEM(full, F32),
            pltpu.VMEM((4 * CHUNKS, channels), F32),
            pltpu.VMEM(full, F32),
            pltpu.VMEM((CHUNKS, channels), BF16),
            pltpu.VMEM((CHUNKS, channels), BF16),
            pltpu.VMEM((STEPS * MODES, channels), F32),
            pltpu.VMEM((STEPS, channels), F32),
            pltpu.VMEM(full, F32),
            pltpu.VMEM(packet, BF16),
            pltpu.VMEM(packet, BF16),
            pltpu.VMEM(packet, BF16),
            pltpu.VMEM(packet, BF16),
            pltpu.SemaphoreType.DMA((5,)),
            pltpu.SemaphoreType.DMA((6,)),
            pltpu.SemaphoreType.DMA((1,)),
        ],
        compiler_params=pltpu.CompilerParams(collective_id=0, has_side_effects=True),
        name="modal_convolution",
    )(qkv, short_filter, decay_rate.T, residue.T, skip.reshape(blocks, LANES))


def solution(mesh):
    in_specs = (P(None, "ch", "seq"), P(None, None, "ch"), P("ch", None), P("ch", None), P("ch"))
    out_specs = P("ch", "seq")
    return jax.shard_map(
        functools.partial(body, mesh.shape["seq"]),
        mesh=mesh,
        in_specs=in_specs,
        out_specs=out_specs,
        check_vma=False,
    )
```

profile of v0, /device:TPU:1, one launch (start us, length us, event | category | flops | bytes accessed | tf_op | source)
XLA Modules:
  0.0 55.1 jit_solution(6844121839200299422)
XLA Ops:
  0.0 52.8 %modal_convolution.1 = bf16[4096,128]{1,0:T(8,128)(2,1)} custom-call(bf16[3,4096,128]{2,1,0:T(8,128)(2,1)} %x_hbm.1, f32[3,3,4096]{2,1,0:T(4,128)} %taps_hbm.1, f32[16,4096]{1,0:T(8,128)} %bitcast.3, f32[16,4096]{1,0:T(8,128)} %bitcast.4, f32[32,128]{1,0:T(8,128)} %bitcast.5), custom_call_target="tpu_custom_call" | custom-call | tf_op jit(solution)/shard_map/modal_convolution/pallas_call | solution.py:344
  52.8 2.3 %copy.7 = bf16[4096,128]{1,0:T(8,128)(2,1)} copy(bf16[4096,128]{1,0:T(8,128)(2,1)} %modal_convolution.1) | data formatting | bytes 2097152
where the time goes:
time: 55.2 us; the launch traced here: 55.1 us
  Pallas kernels  52.8 us (96%)
  local copies, waits for them, and re-layouts  2.26 us (4%)
    pallas_call x1, Pallas kernels, body(): pl.pallas_call(functools.partial(kernel, n), out_shape=jax.ShapeDtypeStru...  52.8 us
    unnamed x1, local copies, waits for them, and re-layouts  2.26 us

commit v1 on v0

--- a/solution.py
+++ b/solution.py
@@ -13,12 +13,21 @@
 LANES = 128
 CHUNKS = 8
 STEPS = 16
+WIDE = 4
+DEEP = 8
+PIECES = 4
+LOCAL_UNROLL = 2
 F32 = jnp.float32
 BF16 = jnp.bfloat16
 
 
 def cols(block):
     return pl.ds(pl.multiple_of(block * LANES, LANES), LANES)
+
+
+def far_first(i, size):
+    half = lax.div(i + 1, 2)
+    return lax.rem(size + size // 2 + jnp.where(lax.rem(i, 2) == 1, half, -half), size)
 
 
 def wide(row):
@@ -43,7 +52,8 @@
     rate_hbm,
     residue_hbm,
     skip_hbm,
-    out_ref,
+    out_hbm,
+    out,
     xv,
     taps,
     rate,
@@ -68,19 +78,38 @@
     load_sems,
     sems,
     own_sem,
+    block_sems,
 ):
     me = lax.axis_index("seq")
     blocks = x_hbm.shape[1] // LANES
     parts = n // blocks
     rows = MODES // parts
     following = lax.rem(me + 1, n)
+    wanted = x_hbm.shape[1] // PIECES
+    row_y = lax.div(me, DEEP * parts)
+    row_z = lax.rem(lax.div(me, parts), DEEP)
+
+    def block_at(z, y):
+        ahead_y = lax.rem(row_y + far_first(y, WIDE), WIDE)
+        ahead_z = lax.rem(row_z + far_first(z, DEEP), DEEP)
+        return ahead_y * DEEP + ahead_z
 
     small = [(rate_hbm, rate), (taps_hbm, taps), (residue_hbm, residue), (skip_hbm, skip)]
     loads = [
         pltpu.make_async_copy(src, dst, load_sems.at[i]) for i, (src, dst) in enumerate(small)
     ]
-    loads.append(pltpu.make_async_copy(x_hbm, xv, load_sems.at[len(small)]))
-    for load in loads:
+
+    def fetch(piece):
+        span = pl.ds(pl.multiple_of(piece * wanted, wanted), wanted)
+        return pltpu.make_async_copy(
+            x_hbm.at[:, span, :], xv.at[:, span, :], load_sems.at[len(small) + piece]
+        )
+
+    for load in loads[:2]:
+        load.start()
+    for piece in range(PIECES):
+        fetch(piece).start()
+    for load in loads[2:]:
         load.start()
 
     barrier = pltpu.get_barrier_semaphore()
@@ -113,8 +142,7 @@
 
     lax.fori_loop(0, blocks, prepare, 0)
 
-    for load in loads[1:]:
-        load.wait()
+    loads[1].wait()
 
     def local(block, carry):
         c = cols(block)
@@ -158,7 +186,16 @@
             states[mode * CHUNKS : (mode + 1) * CHUNKS, c] = state
         return carry
 
-    lax.fori_loop(0, blocks, local, 0)
+    def local_piece(piece, carry):
+        fetch(piece).wait()
+        first_block = piece * (blocks // PIECES)
+        return lax.fori_loop(
+            0, blocks // PIECES, lambda i, v: local(first_block + i, v), carry, unroll=LOCAL_UNROLL
+        )
+
+    lax.fori_loop(0, PIECES, local_piece, 0)
+    for load in loads[2:]:
+        load.wait()
 
     pl.semaphore_wait(barrier, n - 1)
     halo = pltpu.make_async_remote_copy(
@@ -233,35 +270,49 @@
             ).astype(BF16)
         return carry
 
-    lax.fori_loop(0, blocks, finish, 0)
-
-    def exchange(src, dst, send_sem, recv_sem):
-        def one(i, carry):
-            k = lax.rem(me + i, n)
-            pltpu.make_async_remote_copy(
-                src_ref=src.at[k],
-                dst_ref=dst.at[me],
-                send_sem=sems.at[send_sem],
-                recv_sem=sems.at[recv_sem],
-                device_id={"seq": k},
-                device_id_type=MESH,
-            ).start()
-            return carry
-
-        lax.fori_loop(1, n, one, 0)
-        own = pltpu.make_async_copy(src.at[me], dst.at[me], own_sem.at[0])
-        own.start()
-        others = pltpu.make_async_remote_copy(
+    def send_block(src, dst, send_sem, recv_sem, block):
+        for part in range(parts):
+            k = block * parts + part
+
+            @pl.when(k != me)
+            def _():
+                pltpu.make_async_remote_copy(
+                    src_ref=src.at[k],
+                    dst_ref=dst.at[me],
+                    send_sem=sems.at[send_sem],
+                    recv_sem=recv_sem,
+                    device_id={"seq": k},
+                    device_id_type=MESH,
+                ).start()
+
+    def others(src, dst, send_sem, recv_sem):
+        return pltpu.make_async_remote_copy(
             src_ref=src.at[pl.ds(0, n - 1)],
             dst_ref=dst.at[pl.ds(0, n - 1)],
             send_sem=sems.at[send_sem],
-            recv_sem=sems.at[recv_sem],
+            recv_sem=recv_sem,
             device_id={"seq": following},
             device_id_type=MESH,
         )
-        return own, others
-
-    own, others = exchange(ends_out, ends_in, 2, 3)
+
+    def send_ends(z):
+        for y in range(WIDE):
+            send_block(ends_out, ends_in, 2, sems.at[3], block_at(z, y))
+
+    def finish_group(z, carry):
+        for y in range(WIDE):
+            finish(block_at(z, y), 0)
+
+        @pl.when(z > 0)
+        def _():
+            send_ends(z - 1)
+
+        return carry
+
+    lax.fori_loop(0, DEEP, finish_group, 0)
+    send_ends(DEEP - 1)
+    own = pltpu.make_async_copy(ends_out.at[me], ends_in.at[me], own_sem.at[0])
+    own.start()
 
     def inside(block, carry):
         c = cols(block)
@@ -293,17 +344,21 @@
     across = jnp.exp(pick * float(-LANES))
 
     own.wait()
-    others.wait_recv()
+    others(ends_out, ends_in, 2, sems.at[3]).wait_recv()
 
     def carry_on(source, entering):
         starts_out[source] = entering.astype(BF16)
         return across * entering + ends_in[source].astype(F32)
 
     lax.fori_loop(0, n, carry_on, jnp.zeros((rows, LANES), F32), unroll=8)
-    others.wait_send()
-    own, others = exchange(starts_out, starts_in, 4, 5)
-    own.wait()
-    others.wait_recv()
+
+    def send_starts(z, carry):
+        for y in range(WIDE):
+            send_block(starts_out, starts_in, 4, block_sems.at[mine], block_at(z, y))
+        return carry
+
+    lax.fori_loop(0, DEEP, send_starts, 0)
+    pltpu.make_async_copy(starts_out.at[me], starts_in.at[me], block_sems.at[mine]).start()
 
     early = sub.astype(F32) * float(-STEPS)
 
@@ -326,11 +381,38 @@
                 total = total + wide(weights[pl.ds(j * MODES + mode, 1), c]) * entering[mode]
             results.append(feat0[j * CHUNKS : (j + 1) * CHUNKS, c] * rounded(total))
         turned = jnp.concatenate(results, axis=0).T.astype(BF16)
-        out_ref[c, :] = jnp.dot(turned, spread, preferred_element_type=F32).astype(BF16)
-        return carry
-
-    lax.fori_loop(0, blocks, final, 0)
-    others.wait_send()
+        out[c, :] = jnp.dot(turned, spread, preferred_element_type=F32).astype(BF16)
+        return carry
+
+    def put(block):
+        return pltpu.make_async_copy(out.at[cols(block), :], out_hbm.at[cols(block), :], own_sem.at[1])
+
+    def put_group(z):
+        for y in range(WIDE):
+            put(block_at(z, y)).start()
+
+    def final_group(i, carry):
+        z = DEEP - 1 - i
+        for y in range(WIDE):
+            block = block_at(z, y)
+            slots = pl.ds(block * parts, parts)
+            pltpu.make_async_copy(
+                starts_out.at[slots], starts_in.at[slots], block_sems.at[block]
+            ).wait()
+        for y in range(WIDE):
+            final(block_at(z, y), 0)
+
+        @pl.when(i > 0)
+        def _():
+            put_group(z + 1)
+
+        return carry
+
+    lax.fori_loop(0, DEEP, final_group, 0)
+    put_group(0)
+    others(ends_out, ends_in, 2, sems.at[3]).wait_send()
+    others(starts_out, starts_in, 4, sems.at[3]).wait_send()
+    pltpu.make_async_copy(out, out_hbm, own_sem.at[1]).wait()
 
 
 def body(n, qkv, short_filter, decay_rate, residue, skip):
@@ -345,8 +427,9 @@
         functools.partial(kernel, n),
         out_shape=jax.ShapeDtypeStruct((channels, width), BF16),
         in_specs=[anywhere] * 5,
-        out_specs=pl.BlockSpec(memory_space=pltpu.VMEM),
+        out_specs=anywhere,
         scratch_shapes=[
+            pltpu.VMEM((channels, width), BF16),
             pltpu.VMEM(qkv.shape, BF16),
             pltpu.VMEM(short_filter.shape, F32),
             pltpu.VMEM((MODES, channels), F32),
@@ -368,9 +451,10 @@
             pltpu.VMEM(packet, BF16),
             pltpu.VMEM(packet, BF16),
             pltpu.VMEM(packet, BF16),
+            pltpu.SemaphoreType.DMA((4 + PIECES,)),
             pltpu.SemaphoreType.DMA((5,)),
-            pltpu.SemaphoreType.DMA((6,)),
-            pltpu.SemaphoreType.DMA((1,)),
+            pltpu.SemaphoreType.DMA((2,)),
+            pltpu.SemaphoreType.DMA((blocks,)),
         ],
         compiler_params=pltpu.CompilerParams(collective_id=0, has_side_effects=True),
         name="modal_convolution",

time: 55.2 us -> 45.1 us (0.82)
  Pallas kernels: 52.8 us -> 42.8 us
    pallas_call x1, Pallas kernels: 52.8 us -> 42.8 us  [body(): pl.pallas_call(functools.partial(kernel, n), out_shape=jax.ShapeDtypeStru...]
where the time goes in v1:
time: 45.1 us; the launch traced here: 45 us
  Pallas kernels  42.8 us (95%)
  local copies, waits for them, and re-layouts  2.26 us (5%)
    pallas_call x1, Pallas kernels, body(): pl.pallas_call(functools.partial(kernel, n), out_shape=jax.ShapeDtypeStru...  42.8 us
    unnamed x1, local copies, waits for them, and re-layouts  2.26 us

profile of v1, /device:TPU:1, one launch (start us, length us, event | category | flops | bytes accessed | tf_op | source)
XLA Modules:
  0.0 45.0 jit_solution(4880813748568108897)
XLA Ops:
  0.0 42.8 %modal_convolution.1 = bf16[4096,128]{1,0:T(8,128)(2,1)} custom-call(bf16[3,4096,128]{2,1,0:T(8,128)(2,1)} %x_hbm.1, f32[3,3,4096]{2,1,0:T(4,128)} %taps_hbm.1, f32[16,4096]{1,0:T(8,128)} %bitcast.3, f32[16,4096]{1,0:T(8,128)} %bitcast.4, f32[32,128]{1,0:T(8,128)} %bitcast.5), custom_call_target="tpu_custom_call" | custom-call | tf_op jit(solution)/shard_map/modal_convolution/pallas_call | solution.py:426
  42.8 2.3 %copy.7 = bf16[4096,128]{1,0:T(8,128)(2,1)} copy(bf16[4096,128]{1,0:T(8,128)(2,1)} %modal_convolution.1) | data formatting | bytes 2097152

commit v2 on v1

--- a/solution.py
+++ b/solution.py
@@ -17,6 +17,8 @@
 DEEP = 8
 PIECES = 4
 LOCAL_UNROLL = 2
+TURN_UNROLL = 4
+BEFORE = 8
 F32 = jnp.float32
 BF16 = jnp.bfloat16
 
@@ -66,8 +68,12 @@
     states,
     first,
     feat0,
+    turned,
+    entry_scale,
     halo_out,
     halo_in,
+    halo0_out,
+    halo0_in,
     weights,
     near_taps,
     near,
@@ -102,9 +108,12 @@
     def fetch(piece):
         span = pl.ds(pl.multiple_of(piece * wanted, wanted), wanted)
         return pltpu.make_async_copy(
-            x_hbm.at[:, span, :], xv.at[:, span, :], load_sems.at[len(small) + piece]
+            x_hbm.at[pl.ds(1, 2), span, :],
+            xv.at[pl.ds(1, 2), span, :],
+            load_sems.at[len(small) + 1 + piece],
         )
 
+    loads.append(pltpu.make_async_copy(x_hbm.at[0], xv.at[0], load_sems.at[len(small)]))
     for load in loads[:2]:
         load.start()
     for piece in range(PIECES):
@@ -114,13 +123,27 @@
 
     barrier = pltpu.get_barrier_semaphore()
 
-    def greet(i, carry):
-        pl.semaphore_signal(
-            barrier, inc=1, device_id={"seq": lax.rem(me + i, n)}, device_id_type=MESH
-        )
-        return carry
-
-    lax.fori_loop(1, n, greet, 0)
+    def everyone_else(visit):
+        def row(z, carry):
+            for y in range(WIDE):
+                for part in range(parts):
+                    visit(block_at(z, y) * parts + part)
+            return carry
+
+        lax.fori_loop(0, DEEP - 1, row, 0)
+        near_by(visit)
+
+    def near_by(visit):
+        for y in range(WIDE - 1):
+            for part in range(parts):
+                visit(block_at(DEEP - 1, y) * parts + part)
+        for part in range(1, parts):
+            visit(me - lax.rem(me, parts) + lax.rem(me + part, parts))
+
+    def greet(k):
+        pl.semaphore_signal(barrier, inc=1, device_id={"seq": k}, device_id_type=MESH)
+
+    everyone_else(greet)
 
     sub = lax.broadcasted_iota(jnp.int32, (CHUNKS, LANES), 0)
     top = sub == 0
@@ -130,51 +153,98 @@
         token == lax.rem(place, CHUNKS) * STEPS + lax.div(place, CHUNKS), 1.0, 0.0
     ).astype(BF16)
 
+    def turn(stream, c):
+        moved = lax.dot_general(
+            spread, xv[stream, c, :], (((1,), (1,)), ((), ())), preferred_element_type=F32
+        )
+        return [moved[j * CHUNKS : (j + 1) * CHUNKS] for j in range(STEPS)]
+
+    def tails(streams):
+        rows_of = jnp.zeros((CHUNKS, LANES), F32)
+        for i, v in enumerate(streams):
+            for k in range(2):
+                row = 2 * i + k
+                rows_of = jnp.where(sub == row, pltpu.roll(v[14 + k], row + 1, 0), rows_of)
+        return rows_of[0:4].astype(BF16)
+
+    def filtered(stream, c, v):
+        back1 = jnp.where(top, 0.0, pltpu.roll(v[15], 1, 0))
+        back2 = jnp.where(top, 0.0, pltpu.roll(v[14], 1, 0))
+        v = [back2, back1] + v
+        f = [wide(taps[k, pl.ds(stream, 1), c]) for k in range(3)]
+        return [f[0] * v[j + 2] + f[1] * v[j + 1] + f[2] * v[j] for j in range(STEPS)]
+
+    def from_before(stream, c, h):
+        f1 = taps[1, pl.ds(stream, 1), c]
+        f2 = taps[2, pl.ds(stream, 1), c]
+        return [
+            jnp.where(top, wide(f1 * h[1:2] + f2 * h[0:1]), 0.0),
+            jnp.where(top, wide(f2 * h[1:2]), 0.0),
+        ]
+
+    def spread_out(pair, carry):
+        both = pl.ds(pl.multiple_of(pair * 2 * LANES, 2 * LANES), 2 * LANES)
+        moved = []
+        for i in range(2):
+            moved.append(
+                lax.dot_general(
+                    spread,
+                    xv[i + 1, both, :],
+                    (((1,), (1,)), ((), ())),
+                    preferred_element_type=F32,
+                )
+            )
+            turned[i * LANES : (i + 1) * LANES, both] = moved[i]
+        for half in range(2):
+            halo_out[:, cols(2 * pair + half)] = tails(
+                [
+                    [
+                        moved[i][
+                            j * CHUNKS : (j + 1) * CHUNKS, half * LANES : (half + 1) * LANES
+                        ]
+                        for j in range(STEPS)
+                    ]
+                    for i in range(2)
+                ]
+            )
+        return carry
+
+    def spread_piece(piece, carry):
+        fetch(piece).wait()
+        pairs = blocks // PIECES // 2
+        return lax.fori_loop(
+            0,
+            pairs,
+            lambda i, v: spread_out(piece * pairs + i, v),
+            carry,
+            unroll=TURN_UNROLL,
+        )
+
+    lax.fori_loop(0, PIECES, spread_piece, 0)
+
     loads[0].wait()
+    loads[1].wait()
 
     def prepare(block, carry):
         c = cols(block)
-        r = rate[:, c]
-        decay[:, c] = jnp.exp(-r)
-        decay14[:, c] = jnp.exp(-14.0 * r)
-        decay15[:, c] = jnp.exp(-15.0 * r)
-        return carry
-
-    lax.fori_loop(0, blocks, prepare, 0)
-
-    loads[1].wait()
+        decay[:, c] = jnp.exp(-rate[:, c])
+        return carry
+
+    lax.fori_loop(0, blocks, prepare, 0, unroll=4)
 
     def local(block, carry):
         c = cols(block)
         feats = []
-        halo_rows = jnp.zeros((CHUNKS, LANES), F32)
-        for stream in range(3):
-            moved = lax.dot_general(
-                spread,
-                xv[stream, c, :],
-                (((1,), (1,)), ((), ())),
-                preferred_element_type=F32,
-            )
-            v = [moved[j * CHUNKS : (j + 1) * CHUNKS] for j in range(STEPS)]
+        for i in range(2):
+            v = [
+                turned[i * LANES + j * CHUNKS : i * LANES + (j + 1) * CHUNKS, c]
+                for j in range(STEPS)
+            ]
+            feat = filtered(i + 1, c, v)
             for k in range(2):
-                row = 2 * stream + k
-                halo_rows = jnp.where(
-                    sub == row, pltpu.roll(v[14 + k], row + 1, 0), halo_rows
-                )
-            back1 = jnp.where(top, 0.0, pltpu.roll(v[15], 1, 0))
-            back2 = jnp.where(top, 0.0, pltpu.roll(v[14], 1, 0))
-            v = [back2, back1] + v
-            f = [wide(taps[k, pl.ds(stream, 1), c]) for k in range(3)]
-            feat = [f[0] * v[j + 2] + f[1] * v[j + 1] + f[2] * v[j] for j in range(STEPS)]
-            if stream == 0:
-                for j in range(STEPS):
-                    feat0[j * CHUNKS : (j + 1) * CHUNKS, c] = feat[j]
-            else:
-                for k in range(2):
-                    at = (2 * (stream - 1) + k) * CHUNKS
-                    first[at : at + CHUNKS, c] = feat[k]
-                feats.append(feat)
-        halo_out[:, c] = halo_rows.astype(BF16)
+                at = (2 * i + k) * CHUNKS
+                first[at : at + CHUNKS, c] = feat[k]
+            feats.append(feat)
         g = [rounded(feats[0][j] * feats[1][j]) for j in range(STEPS)]
         for j in range(STEPS):
             gated[j * CHUNKS : (j + 1) * CHUNKS, c] = g[j]
@@ -186,42 +256,35 @@
             states[mode * CHUNKS : (mode + 1) * CHUNKS, c] = state
         return carry
 
-    def local_piece(piece, carry):
-        fetch(piece).wait()
-        first_block = piece * (blocks // PIECES)
-        return lax.fori_loop(
-            0, blocks // PIECES, lambda i, v: local(first_block + i, v), carry, unroll=LOCAL_UNROLL
+    lax.fori_loop(0, BEFORE, local, 0, unroll=LOCAL_UNROLL)
+
+    pl.semaphore_wait(barrier, n - 1)
+
+    def to_following(src, dst, sem):
+        return pltpu.make_async_remote_copy(
+            src_ref=src,
+            dst_ref=dst,
+            send_sem=sems.at[sem],
+            recv_sem=sems.at[sem + 1],
+            device_id={"seq": following},
+            device_id_type=MESH,
         )
 
-    lax.fori_loop(0, PIECES, local_piece, 0)
-    for load in loads[2:]:
-        load.wait()
-
-    pl.semaphore_wait(barrier, n - 1)
-    halo = pltpu.make_async_remote_copy(
-        src_ref=halo_out,
-        dst_ref=halo_in,
-        send_sem=sems.at[0],
-        recv_sem=sems.at[1],
-        device_id={"seq": following},
-        device_id_type=MESH,
-    )
+    halo = to_following(halo_out, halo_in, 0)
     halo.start()
-
-    def tables(block, carry):
-        c = cols(block)
-        r = rate[:, c]
+    lax.fori_loop(BEFORE, blocks, local, 0, unroll=LOCAL_UNROLL)
+
+    def powers(block, carry):
+        c = cols(block)
         a = decay[:, c]
-        w = residue[:, c] * jnp.sqrt(one_minus_exp(2.0 * r))
-        direct = skip[pl.ds(block, 1), :]
-        for j in range(STEPS):
-            near_taps[pl.ds(j, 1), c] = jnp.sum(w, axis=0, keepdims=True) + direct
-            direct = 0.0
-            w = w * a
-            weights[j * MODES : (j + 1) * MODES, c] = w
-        return carry
-
-    lax.fori_loop(0, blocks, tables, 0)
+        a2 = a * a
+        a4 = a2 * a2
+        a14 = a4 * a4 * a4 * a2
+        decay14[:, c] = a14
+        decay15[:, c] = a14 * a
+        return carry
+
+    lax.fori_loop(0, blocks, powers, 0, unroll=4)
     halo.wait()
 
     late = (CHUNKS - 1 - sub).astype(F32) * float(-STEPS)
@@ -230,23 +293,12 @@
         c = cols(block)
         h = jnp.where(me == 0, 0.0, halo_in[:, c].astype(F32))
 
-        def add_first(stream):
-            f1 = taps[1, pl.ds(stream, 1), c]
-            f2 = taps[2, pl.ds(stream, 1), c]
-            h2 = h[2 * stream : 2 * stream + 1]
-            h1 = h[2 * stream + 1 : 2 * stream + 2]
-            return [
-                jnp.where(top, wide(f1 * h1 + f2 * h2), 0.0),
-                jnp.where(top, wide(f2 * h1), 0.0),
-            ]
-
-        more = [add_first(stream) for stream in range(3)]
+        more = [from_before(i + 1, c, h[2 * i : 2 * i + 2]) for i in range(2)]
         change = []
         for k in range(2):
             at = slice(k * CHUNKS, (k + 1) * CHUNKS)
-            feat0[at, c] = feat0[at, c] + more[0][k]
-            one = first[k * CHUNKS : (k + 1) * CHUNKS, c] + more[1][k]
-            two = first[(2 + k) * CHUNKS : (3 + k) * CHUNKS, c] + more[2][k]
+            one = first[k * CHUNKS : (k + 1) * CHUNKS, c] + more[0][k]
+            two = first[(2 + k) * CHUNKS : (3 + k) * CHUNKS, c] + more[1][k]
             g = rounded(one * two)
             change.append(g - gated[at, c])
             gated[at, c] = g
@@ -270,20 +322,18 @@
             ).astype(BF16)
         return carry
 
-    def send_block(src, dst, send_sem, recv_sem, block):
-        for part in range(parts):
-            k = block * parts + part
-
-            @pl.when(k != me)
-            def _():
-                pltpu.make_async_remote_copy(
-                    src_ref=src.at[k],
-                    dst_ref=dst.at[me],
-                    send_sem=sems.at[send_sem],
-                    recv_sem=recv_sem,
-                    device_id={"seq": k},
-                    device_id_type=MESH,
-                ).start()
+    def sender(src, dst, send_sem, recv_sem):
+        def send(k):
+            pltpu.make_async_remote_copy(
+                src_ref=src.at[k],
+                dst_ref=dst.at[me],
+                send_sem=sems.at[send_sem],
+                recv_sem=recv_sem,
+                device_id={"seq": k},
+                device_id_type=MESH,
+            ).start()
+
+        return send
 
     def others(src, dst, send_sem, recv_sem):
         return pltpu.make_async_remote_copy(
@@ -295,9 +345,7 @@
             device_id_type=MESH,
         )
 
-    def send_ends(z):
-        for y in range(WIDE):
-            send_block(ends_out, ends_in, 2, sems.at[3], block_at(z, y))
+    send_end = sender(ends_out, ends_in, 2, sems.at[3])
 
     def finish_group(z, carry):
         for y in range(WIDE):
@@ -305,14 +353,51 @@
 
         @pl.when(z > 0)
         def _():
-            send_ends(z - 1)
+            for y in range(WIDE):
+                for part in range(parts):
+                    send_end(block_at(z - 1, y) * parts + part)
 
         return carry
 
     lax.fori_loop(0, DEEP, finish_group, 0)
-    send_ends(DEEP - 1)
+    near_by(send_end)
     own = pltpu.make_async_copy(ends_out.at[me], ends_in.at[me], own_sem.at[0])
     own.start()
+
+    loads[4].wait()
+
+    def query(block, carry):
+        c = cols(block)
+        v = turn(0, c)
+        halo0_out[:, c] = tails([v])
+        feat = filtered(0, c, v)
+        for j in range(STEPS):
+            feat0[j * CHUNKS : (j + 1) * CHUNKS, c] = feat[j]
+        return carry
+
+    lax.fori_loop(0, blocks, query, 0, unroll=2)
+    halo0 = to_following(halo0_out, halo0_in, 5)
+    halo0.start()
+    loads[2].wait()
+    loads[3].wait()
+
+    def tables(block, carry):
+        c = cols(block)
+        r = rate[:, c]
+        a = decay[:, c]
+        w = residue[:, c] * jnp.sqrt(one_minus_exp(2.0 * r))
+        direct = skip[pl.ds(block, 1), :]
+        for j in range(STEPS):
+            near_taps[pl.ds(j, 1), c] = jnp.sum(w, axis=0, keepdims=True) + direct
+            direct = 0.0
+            w = w * a
+            if j == 0:
+                weights[:, c] = w
+        return carry
+
+    lax.fori_loop(0, blocks, tables, 0)
+
+    early = sub.astype(F32) * float(-STEPS)
 
     def inside(block, carry):
         c = cols(block)
@@ -330,7 +415,9 @@
             for shift in (1, 2, 4):
                 state = state + jnp.where(sub < shift, 0.0, step * pltpu.roll(state, shift, 0))
                 step = step * step
-            states[at, c] = jnp.where(top, 0.0, pltpu.roll(state, 1, 0))
+            w = wide(weights[pl.ds(mode, 1), c])
+            states[at, c] = jnp.where(top, 0.0, w * pltpu.roll(state, 1, 0))
+            entry_scale[at, c] = w * jnp.exp(wide(rate[pl.ds(mode, 1), c]) * early)
         return carry
 
     lax.fori_loop(0, blocks, inside, 0)
@@ -352,15 +439,10 @@
 
     lax.fori_loop(0, n, carry_on, jnp.zeros((rows, LANES), F32), unroll=8)
 
-    def send_starts(z, carry):
-        for y in range(WIDE):
-            send_block(starts_out, starts_in, 4, block_sems.at[mine], block_at(z, y))
-        return carry
-
-    lax.fori_loop(0, DEEP, send_starts, 0)
+    everyone_else(sender(starts_out, starts_in, 4, block_sems.at[mine]))
     pltpu.make_async_copy(starts_out.at[me], starts_in.at[me], block_sems.at[mine]).start()
 
-    early = sub.astype(F32) * float(-STEPS)
+    halo0.wait()
 
     def final(block, carry):
         c = cols(block)
@@ -371,17 +453,23 @@
                 group = starts_in[block * parts + mode // rows].astype(F32)
             row = mode % rows
             entering.append(
-                states[at, c]
-                + wide(group[row : row + 1]) * jnp.exp(wide(rate[pl.ds(mode, 1), c]) * early)
+                states[at, c] + wide(group[row : row + 1]) * entry_scale[at, c]
             )
+        before = from_before(0, c, jnp.where(me == 0, 0.0, halo0_in[:, c].astype(F32)))
+        falls = [wide(decay[pl.ds(mode, 1), c]) for mode in range(MODES)]
         results = []
         for j in range(STEPS):
             total = near[j * CHUNKS : (j + 1) * CHUNKS, c]
             for mode in range(MODES):
-                total = total + wide(weights[pl.ds(j * MODES + mode, 1), c]) * entering[mode]
-            results.append(feat0[j * CHUNKS : (j + 1) * CHUNKS, c] * rounded(total))
-        turned = jnp.concatenate(results, axis=0).T.astype(BF16)
-        out[c, :] = jnp.dot(turned, spread, preferred_element_type=F32).astype(BF16)
+                total = total + entering[mode]
+            if j < STEPS - 1:
+                entering = [entering[mode] * falls[mode] for mode in range(MODES)]
+            query_here = feat0[j * CHUNKS : (j + 1) * CHUNKS, c]
+            if j < 2:
+                query_here = query_here + before[j]
+            results.append(query_here * rounded(total))
+        whole = jnp.concatenate(results, axis=0).T.astype(BF16)
+        out[c, :] = jnp.dot(whole, spread, preferred_element_type=F32).astype(BF16)
         return carry
 
     def put(block):
@@ -423,7 +511,7 @@
     anywhere = pl.BlockSpec(memory_space=pl.ANY)
     full = (LANES, channels)
     packet = (n, rows, LANES)
-    return pl.pallas_call(
+    result = pl.pallas_call(
         functools.partial(kernel, n),
         out_shape=jax.ShapeDtypeStruct((channels, width), BF16),
         in_specs=[anywhere] * 5,
@@ -442,23 +530,63 @@
             pltpu.VMEM(full, F32),
             pltpu.VMEM((4 * CHUNKS, channels), F32),
             pltpu.VMEM(full, F32),
-            pltpu.VMEM((CHUNKS, channels), BF16),
-            pltpu.VMEM((CHUNKS, channels), BF16),
-            pltpu.VMEM((STEPS * MODES, channels), F32),
+            pltpu.VMEM((2 * LANES, channels), F32),
+            pltpu.VMEM(full, F32),
+            pltpu.VMEM((4, channels), BF16),
+            pltpu.VMEM((4, channels), BF16),
+            pltpu.VMEM((4, channels), BF16),
+            pltpu.VMEM((4, channels), BF16),
+            pltpu.VMEM((MODES, channels), F32),
             pltpu.VMEM((STEPS, channels), F32),
             pltpu.VMEM(full, F32),
             pltpu.VMEM(packet, BF16),
             pltpu.VMEM(packet, BF16),
             pltpu.VMEM(packet, BF16),
             pltpu.VMEM(packet, BF16),
-            pltpu.SemaphoreType.DMA((4 + PIECES,)),
-            pltpu.SemaphoreType.DMA((5,)),
+            pltpu.SemaphoreType.DMA((5 + PIECES,)),
+            pltpu.SemaphoreType.DMA((7,)),
             pltpu.SemaphoreType.DMA((2,)),
             pltpu.SemaphoreType.DMA((blocks,)),
         ],
         compiler_params=pltpu.CompilerParams(collective_id=0, has_side_effects=True),
         name="modal_convolution",
     )(qkv, short_filter, decay_rate.T, residue.T, skip.reshape(blocks, LANES))
+    return settled(result)
+
+
+def hand_over(src, dst, held, sems):
+    rows = src.shape[0] // PIECES
+    moves = []
+    for piece in range(PIECES):
+        span = pl.ds(piece * rows, rows)
+        moves.append(
+            (
+                pltpu.make_async_copy(src.at[span, :], held.at[span, :], sems.at[0, piece]),
+                pltpu.make_async_copy(held.at[span, :], dst.at[span, :], sems.at[1, piece]),
+            )
+        )
+    for into, _ in moves:
+        into.start()
+    for into, out in moves:
+        into.wait()
+        out.start()
+    for _, out in moves:
+        out.wait()
+
+
+def settled(array):
+    anywhere = pl.BlockSpec(memory_space=pl.ANY)
+    return pl.pallas_call(
+        hand_over,
+        out_shape=jax.ShapeDtypeStruct(array.shape, array.dtype),
+        in_specs=[anywhere],
+        out_specs=anywhere,
+        scratch_shapes=[
+            pltpu.VMEM(array.shape, array.dtype),
+            pltpu.SemaphoreType.DMA((2, PIECES)),
+        ],
+        name="hand_over",
+    )(array)
 
 
 def solution(mesh):

time: 45.1 us -> 40.2 us (0.89)
  Pallas kernels: 42.8 us -> 40.1 us
  local copies, waits for them, and re-layouts: 2.26 us -> 0 us
    pallas_call x1, Pallas kernels: 42.8 us -> 38.1 us  [body(): pl.pallas_call(functools.partial(kernel, n), out_shape=jax.ShapeDtypeStru...]
    unnamed x1 -> x0, local copies, waits for them, and re-layouts: 2.26 us -> none
    pallas_call x0 -> x1, Pallas kernels: none -> 1.98 us  [settled(): pl.pallas_call(hand_over, out_shape=jax.ShapeDtypeStruct(array.shape, arr...]
where the time goes in v2:
time: 40.2 us; the launch traced here: 40.1 us
  Pallas kernels  40.1 us (100%)
    pallas_call x1, Pallas kernels, body(): pl.pallas_call(functools.partial(kernel, n), out_shape=jax.ShapeDtypeStru...  38.1 us
    pallas_call x1, Pallas kernels, settled(): pl.pallas_call(hand_over, out_shape=jax.ShapeDtypeStruct(array.shape, arr...  1.98 us

profile of v2, /device:TPU:1, one launch (start us, length us, event | category | flops | bytes accessed | tf_op | source)
XLA Modules:
  0.0 40.1 jit_solution(11793487311876674209)
XLA Ops:
  0.0 38.1 %modal_convolution.1.src = bf16[4096,128]{1,0:T(8,128)(2,1)} custom-call(bf16[3,4096,128]{2,1,0:T(8,128)(2,1)} %x_hbm.1, f32[3,3,4096]{2,1,0:T(4,128)} %taps_hbm.1, f32[16,4096]{1,0:T(8,128)} %bitcast.3, f32[16,4096]{1,0:T(8,128)} %bitcast.4, f32[32,128]{1,0:T(8,128)} %bitcast.5), custom_call_target="tpu_custom_call" | custom-call | tf_op jit(solution)/shard_map/modal_convolution/pallas_call | solution.py:514
  38.1 2.0 %hand_over.1 = bf16[4096,128]{1,0:T(8,128)(2,1)} custom-call(bf16[4096,128]{1,0:T(8,128)(2,1)} %modal_convolution.1.src), custom_call_target="tpu_custom_call" | custom-call | tf_op jit(solution)/shard_map/hand_over/pallas_call | solution.py:579
